TPU v7x, 256 devices: a whole 4x4x8 slice. The times are simulated.
256 devices in a mesh: group: 16 (over z_lo, y), tok: 16 (over z_hi, x, core).
Axes of the slice: x: 4, y: 4, z: 8 (z_hi: 2, z_lo: 4; z = z_hi * 4 + z_lo), core: 2. Of those that a mesh axis runs over, the one named last changes fastest.
Arguments:
- tokens: bfloat16 [131072, 2048], P(('group', 'tok')), may hold values from -94 to 94
- learning_rates: float32 [2, 131072], P(None, 'group'), may hold values from 0.1 to 1
- channel_gains: float32 [2, 5, 2048], P(None, None, 'tok'), may hold values from 0.3 to 3
- fast_init: float32 [2, 3, 16, 128, 128], P(None, None, 'tok'), may hold values from -0.5 to 0.5
- step_size: float32 [2, 16], P(None, 'tok'), may hold values from 0.05 to 1
- update_table: int32 [2, 16], replicated, may hold values 0 or 1
Outputs:
- mixed: bfloat16 [131072, 2048], P(('group', 'tok'))
All inputs are finite; a program needn't handle non-finite values.
Results may differ from a plain program's by a relative error of at most 0.033.
Values may be sent and summed in bfloat16 or wider, within the bound.
No kernel may reach another device: no remote copies, remote signals or barrier semaphores. Data moves between devices by JAX's collectives and lax.ppermute only.
A program may use at most 64 MiB of HBM per device.

v0:
```python
import functools

import jax
import jax.numpy as jnp
from jax import lax
from jax.experimental import pallas as pl
from jax.experimental.pallas import tpu as pltpu
from jax.sharding import PartitionSpec as P

NS_STEPS = 5
MUON_A = 3.4445
MUON_B = -4.775
MUON_C = 2.0315
EPSILON = 1e-06
CODES = 32767.0
LANES = 128

bf16 = jnp.bfloat16
f32 = jnp.float32


def on_chip():
    return pl.BlockSpec(memory_space=pltpu.VMEM)


def params(mebibytes):
    return pltpu.CompilerParams(vmem_limit_bytes=mebibytes * 1024 * 1024)


def dot(left, right):
    return jnp.dot(left, right, preferred_element_type=f32)


def two_parts(value):
    high = value.astype(bf16)
    return high, (value - high.astype(f32)).astype(bf16)


def dot_parts(left, right):
    (lh, ll), (rh, rl) = left, right
    width = rh.shape[1]
    weights = jnp.concatenate(
        [jnp.concatenate([rh, rl], axis=1), jnp.concatenate([rh, jnp.zeros_like(rl)], axis=1)], axis=0
    )
    both = dot(jnp.concatenate([lh, ll], axis=1), weights)
    return both[:, :width] + both[:, width:]


def gram(parts):
    high, low = parts
    rows = jnp.concatenate(
        [jnp.concatenate([high, high], axis=1), jnp.concatenate([low, jnp.zeros_like(low)], axis=1)], axis=0
    )
    both = lax.dot_general(
        jnp.concatenate([high, low], axis=1), rows, (((1,), (1,)), ((), ())), preferred_element_type=f32
    )
    return both[:, : high.shape[0]] + both[:, high.shape[0] :]


def orthogonalize(gradients):
    current = [
        g * lax.rsqrt(jnp.sum(jnp.sum(g * g, axis=1, keepdims=True), axis=0, keepdims=True) + EPSILON)
        for g in gradients
    ]
    for _ in range(NS_STEPS):
        parts = [two_parts(x) for x in current]
        square = [gram(p) for p in parts]
        halves = [two_parts(s) for s in square]
        polynom = [MUON_B * s + MUON_C * dot_parts(h, h) for s, h in zip(square, halves)]
        current = [
            MUON_A * x + dot_parts(two_parts(q), p) for x, q, p in zip(current, polynom, parts)
        ]
    return current


def moved_on(weights, step, direction, axis):
    moved = weights + step * direction
    before = jnp.sqrt(jnp.sum(weights * weights, axis=axis, keepdims=True) + EPSILON)
    after = jnp.sqrt(jnp.sum(moved * moved, axis=axis, keepdims=True) + EPSILON)
    return moved * (before / after)


def encode(weights, inverse_unit):
    codes = jnp.clip(jnp.round(weights * inverse_unit), -CODES, CODES)
    return codes.astype(jnp.int32).astype(jnp.int16)


def decode(codes, unit):
    return codes.astype(jnp.int32).astype(f32) * unit


def setup_body(slack, init_ref, code_ref, unit_ref, inverse_ref):
    for index in range(init_ref.shape[0]):
        weights = init_ref[index]
        down = index % 3 == 2
        if down:
            weights = weights.T
        total = jnp.sum(weights * weights, axis=1 if down else 0, keepdims=True) + slack
        unit = jnp.broadcast_to(jnp.sqrt(total) * (1.001 / CODES), weights.shape)
        inverse = 1.0 / unit
        unit_ref[index] = unit
        inverse_ref[index] = inverse
        code_ref[index] = encode(weights, inverse)


def setup(fast_init, groups):
    flat = fast_init.reshape((-1,) + fast_init.shape[-2:])
    return pl.pallas_call(
        functools.partial(setup_body, (groups + 2) * EPSILON),
        out_shape=(
            jax.ShapeDtypeStruct(flat.shape, jnp.int16),
            jax.ShapeDtypeStruct(flat.shape, f32),
            jax.ShapeDtypeStruct(flat.shape, f32),
        ),
        in_specs=[on_chip()],
        out_specs=(on_chip(),) * 3,
        compiler_params=params(20),
        name="setup",
    )(flat)


def pack_body(x_ref, o_ref):
    rows, width = x_ref.shape
    heads = width // LANES
    total = jnp.zeros((rows, LANES), f32)
    for head in range(heads):
        piece = x_ref[:, head * LANES : (head + 1) * LANES]
        o_ref[head, :rows, :] = piece
        wide = piece.astype(f32)
        total = total + wide * wide
    lines = [
        jnp.sum(total[r * LANES : (r + 1) * LANES].T, axis=0, keepdims=True) for r in range(rows // LANES)
    ]
    inverse = lax.rsqrt(jnp.concatenate(lines, axis=0) / width + EPSILON)
    high = inverse.astype(bf16).astype(f32)
    middle = (inverse - high).astype(bf16).astype(f32)
    low = inverse - high - middle
    tail = jnp.concatenate([high, middle, low, jnp.zeros_like(low)], axis=0).astype(bf16)
    for head in range(heads):
        o_ref[head, rows:, :] = tail


def pack(x):
    rows, width = x.shape
    tail = 4 * (rows // LANES)
    return pl.pallas_call(
        pack_body,
        out_shape=jax.ShapeDtypeStruct((width // LANES, rows + tail, LANES), bf16),
        compiler_params=params(20),
        name="pack",
    )(x)


def column_of(lines):
    count = lines.shape[0]
    return jnp.concatenate([lines] * (8 // count), axis=0).T


def prep_body(inverse_inside, rows, *refs):
    if inverse_inside:
        x_ref, rate_ref, gain_ref, early_ref, late_ref, inverse_out = refs
    else:
        x_ref, inverse_ref, rate_ref, gain_ref, early_ref, late_ref = refs
    lines = rows // LANES
    norm, key, value = gain_ref[0:1, :], gain_ref[2:3, :], gain_ref[3:4, :]

    def fill(o_ref):
        for block in range(x_ref.shape[0]):
            if inverse_inside:
                tail = x_ref[block, rows:, :].astype(f32)
                inverse = tail[:lines] + tail[lines : 2 * lines] + tail[2 * lines : 3 * lines]
                inverse_out[block] = inverse
            else:
                inverse = inverse_ref[block]
            inverse = column_of(inverse)
            rate = column_of(rate_ref[block])
            for r in range(lines):
                at = block * rows + r * LANES
                wide = x_ref[block, r * LANES : (r + 1) * LANES, :].astype(f32)
                normed = wide * inverse[:, r : r + 1] * norm
                o_ref[0, at : at + LANES, :] = (normed * key).astype(bf16)
                values = (normed * value).astype(bf16)
                o_ref[1, at : at + LANES, :] = (rate[:, r : r + 1] * values.astype(f32)).astype(bf16)

    half = pl.num_programs(0) // 2

    @pl.when(pl.program_id(0) < half)
    def _():
        fill(early_ref)

    @pl.when(pl.program_id(0) >= half)
    def _():
        fill(late_ref)


def prep(x, inverse, rates, gains, rows):
    blocks, height = x.shape[:2]
    lines = rows // LANES
    step = 8
    half = blocks // step // 2
    pair = jax.ShapeDtypeStruct((2, blocks * rows // 2, LANES), bf16)
    line_spec = pl.BlockSpec((step, lines, LANES), lambda i: (i, 0, 0))
    inside = inverse is None
    shapes = [pair, pair]
    out_specs = [
        pl.BlockSpec((2, step * rows, LANES), lambda i: (0, jnp.minimum(i, half - 1), 0)),
        pl.BlockSpec((2, step * rows, LANES), lambda i: (0, jnp.maximum(i - half, 0), 0)),
    ]
    operands = [x, rates, gains] if inside else [x, inverse, rates, gains]
    in_specs = [pl.BlockSpec((step, height, LANES), lambda i: (i, 0, 0))]
    in_specs += [line_spec] * (len(operands) - 2) + [pl.BlockSpec(gains.shape, lambda i: (0, 0))]
    if inside:
        shapes.append(jax.ShapeDtypeStruct((blocks, lines, LANES), f32))
        out_specs.append(line_spec)
    return pl.pallas_call(
        functools.partial(prep_body, inside, rows),
        out_shape=tuple(shapes),
        grid=(blocks // step,),
        in_specs=in_specs,
        out_specs=tuple(out_specs),
        compiler_params=params(40),
        name="prep",
    )(*operands)


def tick_body(chunk, flag_ref, step_ref, w_ref, unit_ref, inverse_ref, early_ref, late_far, o_ref, kept_ref, late_ref, late_sem):
    updates = flag_ref[0] != 0
    late_in = pltpu.make_async_copy(late_far, late_ref, late_sem)

    @pl.when(updates)
    def _():
        late_in.start()


    @pl.when(jnp.logical_not(updates))
    def _():
        o_ref[...] = w_ref[...]
        kept_ref[...] = w_ref[...]

    @pl.when(updates)
    def _():
        weights = [decode(w_ref[j], unit_ref[j]) for j in range(3)]
        gate_up = jnp.concatenate(
            [0.5 * weights[0].astype(bf16).astype(f32), 0.5 * weights[1].astype(bf16).astype(f32)], axis=1
        ).astype(bf16)
        down = weights[2].astype(bf16)
        over_tokens = functools.partial(
            lax.dot_general, dimension_numbers=(((0,), (0,)), ((), ())), preferred_element_type=f32
        )

        def part(d_ref, at):
            keys = d_ref[0, at : at + chunk, :]
            targets = d_ref[1, at : at + chunk, :]
            both = dot(keys, gate_up)
            back = dot(targets, down)
            half, half_up = both[:, :LANES], both[:, LANES:]
            bent = jnp.tanh(half)
            slope = half * bent
            act = half + slope
            hidden = (act * half_up).astype(bf16)
            back_up = (back * act).astype(bf16)
            rise = (1.0 + bent) * (1.0 + (half - slope))
            back_gate = (back * half_up * rise).astype(bf16)
            return (
                over_tokens(keys, jnp.concatenate([back_gate, back_up], axis=1)),
                over_tokens(targets, hidden),
            )

        first, second = part(early_ref, 0)
        for d_ref, begin in ((early_ref, chunk), (late_ref, 0)):
            if d_ref is late_ref:
                late_in.wait()
            for at in range(begin, d_ref.shape[1], chunk):
                more_first, more_second = part(d_ref, at)
                first = first + more_first
                second = second + more_second
        direction = orthogonalize([first[:, :LANES], first[:, LANES:], 2.0 * second])
        for j in range(3):
            fresh = moved_on(weights[j], step_ref[0], direction[j], 1 if j == 2 else 0)
            o_ref[j] = encode(fresh, inverse_ref[j])
            kept_ref[j] = w_ref[j]


def tick(flag, step, codes, unit, inverse_unit, early, late):
    far = pl.BlockSpec(memory_space=pltpu.HBM)
    scalar = pl.BlockSpec(memory_space=pltpu.SMEM)
    shape = jax.ShapeDtypeStruct(codes.shape, jnp.int16)
    return pl.pallas_call(
        functools.partial(tick_body, min(2048, early.shape[1])),
        out_shape=(shape, shape),
        in_specs=[scalar, scalar, on_chip(), on_chip(), on_chip(), on_chip(), far],
        out_specs=(on_chip(), on_chip()),
        scratch_shapes=[
            pltpu.VMEM(late.shape, bf16),
            pltpu.SemaphoreType.DMA,
        ],
        compiler_params=params(24),
        name="tick",
    )(flag, step, codes, unit, inverse_unit, early, late)


def mix_body(rows, x_ref, inverse_ref, gain_ref, w_ref, unit_ref, _, o_ref, *part_ref):
    weights = [decode(w_ref[j], unit_ref[j]).astype(bf16) for j in range(3)]
    gate_up = jnp.concatenate(weights[:2], axis=1)
    down = weights[2].T
    query, scale = gain_ref[0:1, :] * gain_ref[1:2, :], gain_ref[4:5, :]
    lines = rows // LANES
    blocks = x_ref.shape[0]
    pieces = []
    for block in range(blocks):
        inverse = column_of(inverse_ref[block])
        for r in range(lines):
            wide = x_ref[block, r * LANES : (r + 1) * LANES, :].astype(f32)
            pieces.append((wide * inverse[:, r : r + 1] * query).astype(bf16))
    both = dot(jnp.concatenate(pieces, axis=0), gate_up)
    gate, up = both[:, :LANES], both[:, LANES:]
    hidden = (gate * (0.5 * jnp.tanh(0.5 * gate) + 0.5) * up).astype(bf16)
    output = dot(hidden, down)
    ones = jnp.ones((2 * LANES, LANES), bf16)
    own = lax.broadcasted_iota(jnp.int32, (LANES, LANES), 0) == lax.broadcasted_iota(jnp.int32, (LANES, LANES), 1)
    for block in range(blocks):
        mixed = (x_ref[block].astype(f32) + scale * output[block * rows : (block + 1) * rows]).astype(bf16)
        o_ref[block] = mixed
        if part_ref:
            square = mixed.astype(f32)
            total = dot(jnp.concatenate(two_parts(square * square), axis=1), ones)
            part_ref[0][block] = jnp.concatenate(
                [
                    jnp.sum(jnp.where(own, total[r * LANES : (r + 1) * LANES], 0.0), axis=0, keepdims=True)
                    for r in range(lines)
                ],
                axis=0,
            )


def mix(x, inverse, gains, codes, unit, after, rows, sums):
    blocks = x.shape[0]
    step = 8
    lines = rows // LANES
    whole = lambda i: (0, 0)
    cube = lambda i: (0, 0, 0)
    moving = lambda i: (i, 0, 0)
    shapes = [(pltpu.HBM if sums else jax.ShapeDtypeStruct)((blocks, rows, LANES), bf16)]
    out_specs = [pl.BlockSpec((step, rows, LANES), moving)]
    if sums:
        shapes.append(jax.ShapeDtypeStruct((blocks, lines, LANES), f32))
        out_specs.append(pl.BlockSpec((step, lines, LANES), moving))
    return pl.pallas_call(
        functools.partial(mix_body, rows),
        out_shape=tuple(shapes),
        grid=(blocks // step,),
        in_specs=[
            pl.BlockSpec((step, rows, LANES), moving),
            pl.BlockSpec((step, lines, LANES), moving),
            pl.BlockSpec(gains.shape, whole),
            pl.BlockSpec(codes.shape, cube),
            pl.BlockSpec(unit.shape, cube),
            pl.BlockSpec(memory_space=pl.ANY),
        ],
        out_specs=tuple(out_specs),
        compiler_params=params(40),
        name="mix",
    )(x, inverse, gains, codes, unit, after)


def unpack_body(x_ref, o_ref):
    for head in range(x_ref.shape[0]):
        o_ref[:, head * LANES : (head + 1) * LANES] = x_ref[head]


def unpack(x):
    heads, rows, lanes = x.shape
    step = min(rows, 128)
    return pl.pallas_call(
        unpack_body,
        out_shape=jax.ShapeDtypeStruct((rows, heads * lanes), x.dtype),
        grid=(rows // step,),
        in_specs=[pl.BlockSpec((heads, step, lanes), lambda i: (0, i, 0))],
        out_specs=pl.BlockSpec((step, heads * lanes), lambda i: (i, 0)),
        compiler_params=params(20),
        name="unpack",
    )(x)


def passed_on(value, index, groups):
    def hop(target):
        return lambda sent: lax.ppermute(sent, "group", [(target - 1, target)])

    return lax.switch(index, [lambda sent: sent] + [hop(target) for target in range(1, groups)], value)


def held_back(state, me, groups):
    row = 4
    targets = list(range(row - 1, groups - row - 1, row))
    if not targets:
        return jnp.zeros((8, LANES), f32)
    source = targets[-1] + row

    def release(state):
        seed = state[0, :8, :].astype(f32)
        return sum(lax.ppermute(seed, "group", [(source, target)]) for target in targets)

    joins = functools.reduce(jnp.logical_or, [me == group for group in targets + [source]])
    return lax.cond(joins, release, lambda state: jnp.zeros((8, LANES), f32), state)


def summed_over(value, axis):
    size = lax.axis_size(axis)
    bit = 1
    while bit < size:
        value = value + lax.ppermute(value, axis, [(i, i ^ bit) for i in range(size)])
        bit *= 2
    return value


def body(tokens, learning_rates, channel_gains, fast_init, step_size, update_table):
    groups = lax.axis_size("group")
    ranks = lax.axis_size("tok")
    me = lax.axis_index("group")
    rows, width = tokens.shape
    layers = fast_init.shape[0]
    lines = rows // LANES

    codes, unit, inverse_unit = setup(fast_init, groups)
    rates = learning_rates.reshape(layers, ranks, lines, LANES)
    stream = lax.all_to_all(pack(tokens), "tok", split_axis=0, concat_axis=0, tiled=True)
    inverse = None

    for layer in range(layers):
        chosen = slice(3 * layer, 3 * layer + 3)
        stream = pltpu.with_memory_space_constraint(stream, pltpu.HBM)
        prepared = prep(stream, inverse, rates[layer], channel_gains[layer], rows)
        if inverse is None:
            inverse = prepared[2]
        early = pltpu.with_memory_space_constraint(prepared[0], pltpu.VMEM)
        late = prepared[1]
        flag = lax.dynamic_slice(update_table[layer], (me,), (1,))
        flag = jnp.where(me < groups - 1, flag, 0)
        step = step_size[layer]
        layer_unit, layer_inverse = unit[chosen], inverse_unit[chosen]

        def one(index, held):
            arrived = passed_on(held[0], index, groups)
            return lax.cond(
                index == me,
                lambda now, _: tick(flag, step, now, layer_unit, layer_inverse, early, late),
                lambda now, before: (now, before),
                arrived,
                held[1],
            )

        first = codes[chosen]
        _, entering = lax.fori_loop(me, jnp.minimum(me + 2, groups), one, (first, first))
        last = layer + 1 == layers
        after = held_back(entering, me, groups) if last else jnp.zeros((8, LANES), f32)
        outcome = mix(stream, inverse, channel_gains[layer], entering, layer_unit, after, rows, not last)
        stream = outcome[0]
        if not last:
            inverse = lax.rsqrt(summed_over(outcome[1], "tok") / width + EPSILON)
    return unpack(lax.all_to_all(stream, "tok", split_axis=0, concat_axis=0, tiled=True))


def solution(mesh):
    in_specs = (
        P(("group", "tok"), None),
        P(None, "group"),
        P(None, None, "tok"),
        P(None, None, "tok", None, None),
        P(None, "tok"),
        P(),
    )
    out_specs = P(("group", "tok"), None)
    return jax.shard_map(body, mesh=mesh, in_specs=in_specs, out_specs=out_specs, check_vma=False)
```

profile of v0, /device:TPU:120, one launch (start us, length us, event | category | flops | bytes accessed | tf_op | source)
XLA Modules:
  0.0 318.7 jit_solution(14144043196168208252)
XLA Ops:
  0.0 1.6 copy-done
  1.6 2.1 pack.1
  3.7 8.5 %all-to-all-start = ((bf16[16,528,128]{2,1,0:T(8,128)(2,1)}), bf16[16,528,128]{2,1,0:T(8,128)(2,1)}, u32[]{:S(2)}, u32[]{:S(2)}) async-start(bf16[16,528,128]{2,1,0:T(8,128)(2,1)} %pack.1), calls=%async_computation | async-start | bytes 4325376 | tf_op jit(solution)/shard_map/all_to_all | solution.py:426
  12.2 0.3 setup.1
  12.6 0.6 constant_dynamic-slice_fusion
  13.9 0.6 fusion.6
  14.7 36.0 %all-to-all-done.refs_0_.x_ref = bf16[16,528,128]{2,1,0:T(8,128)(2,1)} async-done(((bf16[16,528,128]{2,1,0:T(8,128)(2,1)}), bf16[16,528,128]{2,1,0:T(8,128)(2,1)}, u32[]{:S(2)}, u32[]{:S(2)}) %all-to-all-start) | async-done | bytes 2162720 | tf_op jit(solution)/shard_map/all_to_all | solution.py:426
  50.7 5.7 %prep.2 = (bf16[2,4096,128]{2,1,0:T(8,128)(2,1)S(1)}, bf16[2,4096,128]{2,1,0:T(8,128)(2,1)}, f32[16,4,128]{2,1,0:T(4,128)S(1)}) custom-call(bf16[16,528,128]{2,1,0:T(8,128)(2,1)} %all-to-all-done.refs_0_.x_ref, f32[16,4,128]{2,1,0:T(4,128)S(1)} %bitcast.19, f32[5,128]{1,0:T(8,128)S(1)} %bitcast.20), custom_call_target="tpu_custom_call" | custom-call | tf_op jit(solution)/shard_map/prep/pallas_call | solution.py:215
  56.4 163.3 %while.123 = (s32[]{:T(128)}, s16[3,128,128]{2,1,0:T(8,128)(2,1)S(1)}, s16[3,128,128]{2,1,0:T(8,128)(2,1)S(1)}, s32[]{:T(128)}, s32[]{:T(128)}, /*index=5*/s32[1...) while((s32[]{:T(128)}, ...), condition=%wide.region_19.20_spmd, body=%wide.region_0.19_spmd.sunk | while | flops 5 | bytes 786723 | solution.py:453
  56.4 162.5 %conditional.10 = (s16[3,128,128]{2,1,0:T(8,128)(2,1)S(1)}) conditional(s32[]{:T(128)} %clamp.8, s16[3,128,128]{2,1,0:T(8,128)(2,1)S(1)} %get-tuple-element.496, s16[3,128,128]{2,1,0:T(8,128)(2,1)S(1)} %get-tuple-element.496, s16[3,128,128]{2,1,0:T(8,128)(2,1)S(1)} %get-tuple-element.496, ...), branch_computations={%region_1.1_spmd, %region_2.2_spmd, %region_3.3_spmd, %region_4.4_... | conditional | bytes 589872 | solution.py:389
  56.4 1.3 collective-permute-start.14
  57.7 161.2 %collective-permute-done.14 = s16[3,128,128]{2,1,0:T(8,128)(2,1)S(1)} collective-permute-done((s16[3,128,128]{2,1,0:T(8,128)(2,1)S(1)}, s16[3,128,128]{2,1,0:T(8,128)(2,1)S(1)}, u32[]{:S(2)}, u32[]{:S(2)}) %collective-permute-start.14) | collective-permute-done | bytes 98336 | tf_op jit(solution)/shard_map/while/body/cond/branch_15_fun/ppermute | solution.py:387
  218.9 0.6 conditional.11
  218.9 0.6 tick.2
  219.7 6.8 %mix.2 = (bf16[16,512,128]{2,1,0:T(8,128)(2,1)}, f32[16,4,128]{2,1,0:T(4,128)S(1)}) custom-call(bf16[16,528,128]{2,1,0:T(8,128)(2,1)} %all-to-all-done.refs_0_.x_ref, f32[16,4,128]{2,1,0:T(4,128)S(1)} %get-tuple-element.255.inverse_ref, f32[5,128]{1,0:T(8,128)S(1)} %bitcast.21, s16[3,128,128]{2,1,0:T(8,128)(2,1)S(1)} %get-tuple-element.261.w_ref, ...), custom_call_target="tpu_custom_call" | custom-call | tf_op jit(solution)/shard_map/mix/pallas_call | solution.py:348
  226.6 1.2 collective-permute-done.32
  227.8 0.1 collective-permute-start.33
  227.9 3.9 %collective-permute-done.33 = f32[16,4,128]{2,1,0:T(4,128)S(1)} collective-permute-done((f32[16,4,128]{2,1,0:T(4,128)S(1)}, f32[16,4,128]{2,1,0:T(4,128)S(1)}, u32[]{:S(2)}, u32[]{:S(2)}) %collective-permute-start.33) | collective-permute-done | bytes 32800 | tf_op jit(solution)/shard_map/ppermute | solution.py:411
  231.8 0.9 collective-permute-start.34
  232.7 4.6 %collective-permute-done.34 = f32[16,4,128]{2,1,0:T(4,128)S(1)} collective-permute-done((f32[16,4,128]{2,1,0:T(4,128)S(1)}, f32[16,4,128]{2,1,0:T(4,128)S(1)}, u32[]{:S(2)}, u32[]{:S(2)}) %collective-permute-start.34) | collective-permute-done | bytes 32800 | tf_op jit(solution)/shard_map/ppermute | solution.py:411
  237.3 0.4 collective-permute-start.35
  238.4 6.8 %collective-permute-done.35 = f32[16,4,128]{2,1,0:T(4,128)S(1)} collective-permute-done((f32[16,4,128]{2,1,0:T(4,128)S(1)}, f32[16,4,128]{2,1,0:T(4,128)S(1)}, u32[]{:S(2)}, u32[]{:S(2)}) %collective-permute-start.35) | collective-permute-done | bytes 32800 | tf_op jit(solution)/shard_map/ppermute | solution.py:411
  245.2 5.7 %prep.3 = (bf16[2,4096,128]{2,1,0:T(8,128)(2,1)S(1)}, bf16[2,4096,128]{2,1,0:T(8,128)(2,1)}) custom-call(bf16[16,512,128]{2,1,0:T(8,128)(2,1)} %get-tuple-element.262.refs_0_.x_ref, f32[16,4,128]{2,1,0:T(4,128)S(1)} %add_rsqrt_fusion.refs_1_.inverse_ref, f32[16,4,128]{2,1,0:T(4,128)S(1)} %bitcast.18, f32[5,128]{1,0:T(8,128)S(1)} %bitcast.22), custom_call_target="tpu_custom_call" | custom-call | tf_op jit(solution)/shard_map/prep/pallas_call | solution.py:215
  251.0 26.1 %while.124 = (s32[]{:T(128)}, s16[3,128,128]{2,1,0:T(8,128)(2,1)S(1)}, s16[3,128,128]{2,1,0:T(8,128)(2,1)S(1)}, s32[]{:T(128)}, s32[]{:T(128)}, /*index=5*/s32[1...) while((s32[]{:T(128)}, ...), condition=%wide.region_39.40_spmd, body=%wide.region_20.39_spmd.sunk | while | flops 5 | bytes 786723 | solution.py:453
  251.0 25.3 %conditional.12 = (s16[3,128,128]{2,1,0:T(8,128)(2,1)S(1)}) conditional(s32[]{:T(128)} %clamp.9, s16[3,128,128]{2,1,0:T(8,128)(2,1)S(1)} %get-tuple-element.538, s16[3,128,128]{2,1,0:T(8,128)(2,1)S(1)} %get-tuple-element.538, s16[3,128,128]{2,1,0:T(8,128)(2,1)S(1)} %get-tuple-element.538, ...), branch_computations={%region_21.21_spmd, %region_22.22_spmd, %region_23.23_spmd, %regio... | conditional | bytes 589872 | solution.py:389
  251.0 1.3 collective-permute-start.29
  252.3 24.0 %collective-permute-done.29 = s16[3,128,128]{2,1,0:T(8,128)(2,1)S(1)} collective-permute-done((s16[3,128,128]{2,1,0:T(8,128)(2,1)S(1)}, s16[3,128,128]{2,1,0:T(8,128)(2,1)S(1)}, u32[]{:S(2)}, u32[]{:S(2)}) %collective-permute-start.29) | collective-permute-done | bytes 98336 | tf_op jit(solution)/shard_map/while/body/cond/branch_15_fun/ppermute | solution.py:387
  276.3 0.7 conditional.13
  276.3 0.7 tick.3
  277.1 4.7 %mix.3 = bf16[16,512,128]{2,1,0:T(8,128)(2,1)S(1)} custom-call(bf16[16,512,128]{2,1,0:T(8,128)(2,1)} %get-tuple-element.262.refs_0_.x_ref, f32[16,4,128]{2,1,0:T(4,128)S(1)} %add_rsqrt_fusion.refs_1_.inverse_ref, f32[5,128]{1,0:T(8,128)S(1)} %bitcast.23, s16[3,128,128]{2,1,0:T(8,128)(2,1)S(1)} %get-tuple-element.266.w_ref, ...), custom_call_target="tpu_custom_call" | custom-call | tf_op jit(solution)/shard_map/mix/pallas_call | solution.py:348
  281.8 34.7 %all_to_all.10.x_ref = bf16[16,512,128]{2,1,0:T(8,128)(2,1)S(1)} all-to-all(bf16[16,512,128]{2,1,0:T(8,128)(2,1)S(1)} %mix.3), channel_id=1, replica_groups=mesh['group'=16,'tok'=16] {'tok'}, dimensions={0} | all-to-all | bytes 4194304 | tf_op jit(solution)/shard_map/all_to_all | solution.py:460
  316.5 2.1 unpack.1
  (32 shorter events, 0.3 us)
Async XLA Ops:
  0.0 1.6 copy-start
  3.7 8.6 %copy-start.1 = (f32[2,3,1,128,128]{4,3,2,1,0:T(8,128)S(1)}, f32[2,3,1,128,128]{4,3,2,1,0:T(8,128)}, u32[]{:S(2)}) copy-start(f32[2,3,1,128,128]{4,3,2,1,0:T(8,128)} %param.51) | copy-start | bytes 1179652
  3.7 8.8 %copy-start.3 = (f32[2,5,128]{2,0,1:T(2,128)S(1)}, f32[2,5,128]{2,0,1:T(2,128)}, u32[]{:S(2)}) copy-start(f32[2,5,128]{2,0,1:T(2,128)} %param.50) | copy-start | bytes 15364
  3.7 8.9 %copy-start.5 = (s32[2,16]{1,0:T(2,128)S(1)}, s32[2,16]{1,0:T(2,128)}, u32[]{:S(2)}) copy-start(s32[2,16]{1,0:T(2,128)} %param.53) | copy-start | bytes 388
  3.7 10.2 %copy-start.4 = (f32[2,1]{0,1:T(1,128)S(1)}, f32[2,1]{0,1:T(1,128)}, u32[]{:S(2)}) copy-start(f32[2,1]{0,1:T(1,128)} %param.52) | copy-start | bytes 28
  3.7 47.0 %all-to-all-start = ((bf16[16,528,128]{2,1,0:T(8,128)(2,1)}), bf16[16,528,128]{2,1,0:T(8,128)(2,1)}, u32[]{:S(2)}, u32[]{:S(2)}) async-start(bf16[16,528,128]{2,1,0:T(8,128)(2,1)} %pack.1), calls=%async_computation | async-start | bytes 4325376 | tf_op jit(solution)/shard_map/all_to_all | solution.py:426
  12.2 2.4 copy-start.2
  56.4 162.5 %collective-permute-start.14 = (s16[3,128,128]{2,1,0:T(8,128)(2,1)S(1)}, s16[3,128,128]{2,1,0:T(8,128)(2,1)S(1)}, u32[]{:S(2)}, u32[]{:S(2)}) collective-permute-start(s16[3,128,128]{2,1,0:T(8,128)(2,1)S(1)} %param.15), channel_id=1, source_target_pairs={{224,240},{225,241},{226,242},{227,243},{228,244},{229,245},{230,2... | collective-permute-start | bytes 294920 | tf_op jit(solution)/shard_map/while/body/cond/branch_15_fun/ppermute | solution.py:387
  226.6 1.2 collective-permute-start.32
  227.8 4.0 %collective-permute-start.33 = (f32[16,4,128]{2,1,0:T(4,128)S(1)}, f32[16,4,128]{2,1,0:T(4,128)S(1)}, u32[]{:S(2)}, u32[]{:S(2)}) collective-permute-start(f32[16,4,128]{2,1,0:T(4,128)S(1)} %add.37), channel_id=1, source_target_pairs={{0,2},{1,3},{2,0},{3,1},{4,6},{5,7},{6,4},{7,5},{8,10},{9,11},{10,... | collective-permute-start | bytes 98312 | tf_op jit(solution)/shard_map/ppermute | solution.py:411
  231.8 5.5 %collective-permute-start.34 = (f32[16,4,128]{2,1,0:T(4,128)S(1)}, f32[16,4,128]{2,1,0:T(4,128)S(1)}, u32[]{:S(2)}, u32[]{:S(2)}) collective-permute-start(f32[16,4,128]{2,1,0:T(4,128)S(1)} %add.38), channel_id=1, source_target_pairs={{0,4},{1,5},{2,6},{3,7},{4,0},{5,1},{6,2},{7,3},{8,12},{9,13},{10,... | collective-permute-start | bytes 98312 | tf_op jit(solution)/shard_map/ppermute | solution.py:411
  237.3 7.9 %collective-permute-start.35 = (f32[16,4,128]{2,1,0:T(4,128)S(1)}, f32[16,4,128]{2,1,0:T(4,128)S(1)}, u32[]{:S(2)}, u32[]{:S(2)}) collective-permute-start(f32[16,4,128]{2,1,0:T(4,128)S(1)} %add.39), channel_id=1, source_target_pairs={{0,8},{1,9},{2,10},{3,11},{4,12},{5,13},{6,14},{7,15},{8,0},{9,1},... | collective-permute-start | bytes 98312 | tf_op jit(solution)/shard_map/ppermute | solution.py:411
  251.0 25.3 %collective-permute-start.29 = (s16[3,128,128]{2,1,0:T(8,128)(2,1)S(1)}, s16[3,128,128]{2,1,0:T(8,128)(2,1)S(1)}, u32[]{:S(2)}, u32[]{:S(2)}) collective-permute-start(s16[3,128,128]{2,1,0:T(8,128)(2,1)S(1)} %param.35), channel_id=1, source_target_pairs={{224,240},{225,241},{226,242},{227,243},{228,244},{229,245},{230,2... | collective-permute-start | bytes 294920 | tf_op jit(solution)/shard_map/while/body/cond/branch_15_fun/ppermute | solution.py:387
where the time goes:
time: 322 us; the launch traced here: 319 us
  waiting for transfers between devices  238 us (74%)
  blocking collectives  34.7 us (11%)
  Pallas kernels  28.7 us (9%)
  starting transfers between devices  12.5 us (4%)
    ppermute x2, waiting for transfers between devices, hop(): return lambda sent: lax.ppermute(sent, 'group', [(target - 1, target)])  185 us
    all_to_all x1, waiting for transfers between devices, body(): lax.all_to_all(pack(tokens), 'tok', split_axis=0, concat_axis=0, tiled=True)  36 us
    all_to_all x1, blocking collectives, body(): lax.all_to_all(stream, 'tok', split_axis=0, concat_axis=0, tiled=True)  34.7 us
    ppermute x4, waiting for transfers between devices, summed_over(): lax.ppermute(value, axis, [(i, i ^ bit) for i in range(size)])  16.5 us
    pallas_call x2, Pallas kernels, mix(): pl.pallas_call(functools.partial(mix_body, rows), out_shape=tuple(shapes)...  11.5 us
    pallas_call x2, Pallas kernels, prep(): pl.pallas_call(functools.partial(prep_body, inside, rows), out_shape=tupl...  11.4 us
    all_to_all x1, starting transfers between devices, body(): lax.all_to_all(pack(tokens), 'tok', split_axis=0, concat_axis=0, tiled=True)  8.52 us
  transfers between devices with their start and end apart: 7, of which 7 were waited for; matrix products, arithmetic and copies ran while one was open for 0% of the time, Pallas kernels for 0%

commit v1 on v0

--- a/solution.py
+++ b/solution.py
@@ -162,7 +162,7 @@
     else:
         x_ref, inverse_ref, rate_ref, gain_ref, early_ref, late_ref = refs
     lines = rows // LANES
-    norm, key, value = gain_ref[0:1, :], gain_ref[2:3, :], gain_ref[3:4, :]
+    key, value = gain_ref[0:1, :] * gain_ref[2:3, :], gain_ref[0:1, :] * gain_ref[3:4, :]
 
     def fill(o_ref):
         for block in range(x_ref.shape[0]):
@@ -177,7 +177,7 @@
             for r in range(lines):
                 at = block * rows + r * LANES
                 wide = x_ref[block, r * LANES : (r + 1) * LANES, :].astype(f32)
-                normed = wide * inverse[:, r : r + 1] * norm
+                normed = wide * inverse[:, r : r + 1]
                 o_ref[0, at : at + LANES, :] = (normed * key).astype(bf16)
                 values = (normed * value).astype(bf16)
                 o_ref[1, at : at + LANES, :] = (rate[:, r : r + 1] * values.astype(f32)).astype(bf16)
@@ -370,7 +370,7 @@
 
 def unpack(x):
     heads, rows, lanes = x.shape
-    step = min(rows, 128)
+    step = min(rows, 256)
     return pl.pallas_call(
         unpack_body,
         out_shape=jax.ShapeDtypeStruct((rows, heads * lanes), x.dtype),

time: 322 us -> 314 us (0.975)
  waiting for transfers between devices: 238 us -> 230 us
    ppermute x2, waiting for transfers between devices: 185 us -> 178 us  [hop(): return lambda sent: lax.ppermute(sent, 'group', [(target - 1, target)])]
where the time goes in v1:
time: 314 us; the launch traced here: 311 us
  waiting for transfers between devices  230 us (73%)
  blocking collectives  34.7 us (11%)
  Pallas kernels  28.3 us (9%)
  starting transfers between devices  12.5 us (4%)
    ppermute x2, waiting for transfers between devices, hop(): return lambda sent: lax.ppermute(sent, 'group', [(target - 1, target)])  178 us
    all_to_all x1, waiting for transfers between devices, body(): lax.all_to_all(pack(tokens), 'tok', split_axis=0, concat_axis=0, tiled=True)  36 us
    all_to_all x1, blocking collectives, body(): lax.all_to_all(stream, 'tok', split_axis=0, concat_axis=0, tiled=True)  34.7 us
    ppermute x4, waiting for transfers between devices, summed_over(): lax.ppermute(value, axis, [(i, i ^ bit) for i in range(size)])  16.5 us
    pallas_call x2, Pallas kernels, mix(): pl.pallas_call(functools.partial(mix_body, rows), out_shape=tuple(shapes)...  11.5 us
    pallas_call x2, Pallas kernels, prep(): pl.pallas_call(functools.partial(prep_body, inside, rows), out_shape=tupl...  11.4 us
    all_to_all x1, starting transfers between devices, body(): lax.all_to_all(pack(tokens), 'tok', split_axis=0, concat_axis=0, tiled=True)  8.52 us
  transfers between devices with their start and end apart: 7, of which 7 were waited for; matrix products, arithmetic and copies ran while one was open for 0% of the time, Pallas kernels for 0%

profile of v1, /device:TPU:120, one launch (start us, length us, event | category | flops | bytes accessed | tf_op | source)
XLA Modules:
  0.0 310.6 jit_solution(5659994793664217348)
XLA Ops:
  0.0 1.6 copy-done
  1.6 2.1 pack.1
  3.7 8.5 %all-to-all-start = ((bf16[16,528,128]{2,1,0:T(8,128)(2,1)}), bf16[16,528,128]{2,1,0:T(8,128)(2,1)}, u32[]{:S(2)}, u32[]{:S(2)}) async-start(bf16[16,528,128]{2,1,0:T(8,128)(2,1)} %pack.1), calls=%async_computation | async-start | bytes 4325376 | tf_op jit(solution)/shard_map/all_to_all | solution.py:426
  12.2 0.3 setup.1
  12.6 0.6 constant_dynamic-slice_fusion
  13.9 0.6 fusion.6
  14.7 36.0 %all-to-all-done.refs_0_.x_ref = bf16[16,528,128]{2,1,0:T(8,128)(2,1)} async-done(((bf16[16,528,128]{2,1,0:T(8,128)(2,1)}), bf16[16,528,128]{2,1,0:T(8,128)(2,1)}, u32[]{:S(2)}, u32[]{:S(2)}) %all-to-all-start) | async-done | bytes 2162720 | tf_op jit(solution)/shard_map/all_to_all | solution.py:426
  50.7 5.7 %prep.2 = (bf16[2,4096,128]{2,1,0:T(8,128)(2,1)S(1)}, bf16[2,4096,128]{2,1,0:T(8,128)(2,1)}, f32[16,4,128]{2,1,0:T(4,128)S(1)}) custom-call(bf16[16,528,128]{2,1,0:T(8,128)(2,1)} %all-to-all-done.refs_0_.x_ref, f32[16,4,128]{2,1,0:T(4,128)S(1)} %bitcast.19, f32[5,128]{1,0:T(8,128)S(1)} %bitcast.20), custom_call_target="tpu_custom_call" | custom-call | tf_op jit(solution)/shard_map/prep/pallas_call | solution.py:215
  56.4 157.1 %while.123 = (s32[]{:T(128)}, s16[3,128,128]{2,1,0:T(8,128)(2,1)S(1)}, s16[3,128,128]{2,1,0:T(8,128)(2,1)S(1)}, s32[]{:T(128)}, s32[]{:T(128)}, /*index=5*/s32[1...) while((s32[]{:T(128)}, ...), condition=%wide.region_19.20_spmd, body=%wide.region_0.19_spmd.sunk | while | flops 5 | bytes 786723 | solution.py:453
  56.4 156.3 %conditional.10 = (s16[3,128,128]{2,1,0:T(8,128)(2,1)S(1)}) conditional(s32[]{:T(128)} %clamp.8, s16[3,128,128]{2,1,0:T(8,128)(2,1)S(1)} %get-tuple-element.496, s16[3,128,128]{2,1,0:T(8,128)(2,1)S(1)} %get-tuple-element.496, s16[3,128,128]{2,1,0:T(8,128)(2,1)S(1)} %get-tuple-element.496, ...), branch_computations={%region_1.1_spmd, %region_2.2_spmd, %region_3.3_spmd, %region_4.4_... | conditional | bytes 589872 | solution.py:389
  56.4 1.3 collective-permute-start.14
  57.7 155.0 %collective-permute-done.14 = s16[3,128,128]{2,1,0:T(8,128)(2,1)S(1)} collective-permute-done((s16[3,128,128]{2,1,0:T(8,128)(2,1)S(1)}, s16[3,128,128]{2,1,0:T(8,128)(2,1)S(1)}, u32[]{:S(2)}, u32[]{:S(2)}) %collective-permute-start.14) | collective-permute-done | bytes 98336 | tf_op jit(solution)/shard_map/while/body/cond/branch_15_fun/ppermute | solution.py:387
  212.7 0.6 conditional.11
  212.7 0.6 tick.2
  213.5 6.8 %mix.2 = (bf16[16,512,128]{2,1,0:T(8,128)(2,1)}, f32[16,4,128]{2,1,0:T(4,128)S(1)}) custom-call(bf16[16,528,128]{2,1,0:T(8,128)(2,1)} %all-to-all-done.refs_0_.x_ref, f32[16,4,128]{2,1,0:T(4,128)S(1)} %get-tuple-element.255.inverse_ref, f32[5,128]{1,0:T(8,128)S(1)} %bitcast.21, s16[3,128,128]{2,1,0:T(8,128)(2,1)S(1)} %get-tuple-element.261.w_ref, ...), custom_call_target="tpu_custom_call" | custom-call | tf_op jit(solution)/shard_map/mix/pallas_call | solution.py:348
  220.3 1.2 collective-permute-done.32
  221.5 0.1 collective-permute-start.33
  221.6 3.9 %collective-permute-done.33 = f32[16,4,128]{2,1,0:T(4,128)S(1)} collective-permute-done((f32[16,4,128]{2,1,0:T(4,128)S(1)}, f32[16,4,128]{2,1,0:T(4,128)S(1)}, u32[]{:S(2)}, u32[]{:S(2)}) %collective-permute-start.33) | collective-permute-done | bytes 32800 | tf_op jit(solution)/shard_map/ppermute | solution.py:411
  225.6 0.9 collective-permute-start.34
  226.5 4.6 %collective-permute-done.34 = f32[16,4,128]{2,1,0:T(4,128)S(1)} collective-permute-done((f32[16,4,128]{2,1,0:T(4,128)S(1)}, f32[16,4,128]{2,1,0:T(4,128)S(1)}, u32[]{:S(2)}, u32[]{:S(2)}) %collective-permute-start.34) | collective-permute-done | bytes 32800 | tf_op jit(solution)/shard_map/ppermute | solution.py:411
  231.1 0.4 collective-permute-start.35
  232.2 6.8 %collective-permute-done.35 = f32[16,4,128]{2,1,0:T(4,128)S(1)} collective-permute-done((f32[16,4,128]{2,1,0:T(4,128)S(1)}, f32[16,4,128]{2,1,0:T(4,128)S(1)}, u32[]{:S(2)}, u32[]{:S(2)}) %collective-permute-start.35) | collective-permute-done | bytes 32800 | tf_op jit(solution)/shard_map/ppermute | solution.py:411
  239.0 5.7 %prep.3 = (bf16[2,4096,128]{2,1,0:T(8,128)(2,1)S(1)}, bf16[2,4096,128]{2,1,0:T(8,128)(2,1)}) custom-call(bf16[16,512,128]{2,1,0:T(8,128)(2,1)} %get-tuple-element.262.refs_0_.x_ref, f32[16,4,128]{2,1,0:T(4,128)S(1)} %add_rsqrt_fusion.refs_1_.inverse_ref, f32[16,4,128]{2,1,0:T(4,128)S(1)} %bitcast.18, f32[5,128]{1,0:T(8,128)S(1)} %bitcast.22), custom_call_target="tpu_custom_call" | custom-call | tf_op jit(solution)/shard_map/prep/pallas_call | solution.py:215
  244.7 24.6 %while.124 = (s32[]{:T(128)}, s16[3,128,128]{2,1,0:T(8,128)(2,1)S(1)}, s16[3,128,128]{2,1,0:T(8,128)(2,1)S(1)}, s32[]{:T(128)}, s32[]{:T(128)}, /*index=5*/s32[1...) while((s32[]{:T(128)}, ...), condition=%wide.region_39.40_spmd, body=%wide.region_20.39_spmd.sunk | while | flops 5 | bytes 786723 | solution.py:453
  244.7 23.9 %conditional.12 = (s16[3,128,128]{2,1,0:T(8,128)(2,1)S(1)}) conditional(s32[]{:T(128)} %clamp.9, s16[3,128,128]{2,1,0:T(8,128)(2,1)S(1)} %get-tuple-element.538, s16[3,128,128]{2,1,0:T(8,128)(2,1)S(1)} %get-tuple-element.538, s16[3,128,128]{2,1,0:T(8,128)(2,1)S(1)} %get-tuple-element.538, ...), branch_computations={%region_21.21_spmd, %region_22.22_spmd, %region_23.23_spmd, %regio... | conditional | bytes 589872 | solution.py:389
  244.7 1.3 collective-permute-start.29
  246.0 22.5 %collective-permute-done.29 = s16[3,128,128]{2,1,0:T(8,128)(2,1)S(1)} collective-permute-done((s16[3,128,128]{2,1,0:T(8,128)(2,1)S(1)}, s16[3,128,128]{2,1,0:T(8,128)(2,1)S(1)}, u32[]{:S(2)}, u32[]{:S(2)}) %collective-permute-start.29) | collective-permute-done | bytes 98336 | tf_op jit(solution)/shard_map/while/body/cond/branch_15_fun/ppermute | solution.py:387
  268.6 0.7 conditional.13
  268.6 0.7 tick.3
  269.4 4.7 %mix.3 = bf16[16,512,128]{2,1,0:T(8,128)(2,1)S(1)} custom-call(bf16[16,512,128]{2,1,0:T(8,128)(2,1)} %get-tuple-element.262.refs_0_.x_ref, f32[16,4,128]{2,1,0:T(4,128)S(1)} %add_rsqrt_fusion.refs_1_.inverse_ref, f32[5,128]{1,0:T(8,128)S(1)} %bitcast.23, s16[3,128,128]{2,1,0:T(8,128)(2,1)S(1)} %get-tuple-element.266.w_ref, ...), custom_call_target="tpu_custom_call" | custom-call | tf_op jit(solution)/shard_map/mix/pallas_call | solution.py:348
  274.1 34.7 %all_to_all.10.x_ref = bf16[16,512,128]{2,1,0:T(8,128)(2,1)S(1)} all-to-all(bf16[16,512,128]{2,1,0:T(8,128)(2,1)S(1)} %mix.3), channel_id=1, replica_groups=mesh['group'=16,'tok'=16] {'tok'}, dimensions={0} | all-to-all | bytes 4194304 | tf_op jit(solution)/shard_map/all_to_all | solution.py:460
  308.8 1.8 unpack.1
  (32 shorter events, 0.3 us)
Async XLA Ops:
  0.0 1.6 copy-start
  3.7 8.6 %copy-start.1 = (f32[2,3,1,128,128]{4,3,2,1,0:T(8,128)S(1)}, f32[2,3,1,128,128]{4,3,2,1,0:T(8,128)}, u32[]{:S(2)}) copy-start(f32[2,3,1,128,128]{4,3,2,1,0:T(8,128)} %param.51) | copy-start | bytes 1179652
  3.7 8.8 %copy-start.3 = (f32[2,5,128]{2,0,1:T(2,128)S(1)}, f32[2,5,128]{2,0,1:T(2,128)}, u32[]{:S(2)}) copy-start(f32[2,5,128]{2,0,1:T(2,128)} %param.50) | copy-start | bytes 15364
  3.7 8.9 %copy-start.5 = (s32[2,16]{1,0:T(2,128)S(1)}, s32[2,16]{1,0:T(2,128)}, u32[]{:S(2)}) copy-start(s32[2,16]{1,0:T(2,128)} %param.53) | copy-start | bytes 388
  3.7 10.2 %copy-start.4 = (f32[2,1]{0,1:T(1,128)S(1)}, f32[2,1]{0,1:T(1,128)}, u32[]{:S(2)}) copy-start(f32[2,1]{0,1:T(1,128)} %param.52) | copy-start | bytes 28
  3.7 47.0 %all-to-all-start = ((bf16[16,528,128]{2,1,0:T(8,128)(2,1)}), bf16[16,528,128]{2,1,0:T(8,128)(2,1)}, u32[]{:S(2)}, u32[]{:S(2)}) async-start(bf16[16,528,128]{2,1,0:T(8,128)(2,1)} %pack.1), calls=%async_computation | async-start | bytes 4325376 | tf_op jit(solution)/shard_map/all_to_all | solution.py:426
  12.2 2.4 copy-start.2
  56.4 156.3 %collective-permute-start.14 = (s16[3,128,128]{2,1,0:T(8,128)(2,1)S(1)}, s16[3,128,128]{2,1,0:T(8,128)(2,1)S(1)}, u32[]{:S(2)}, u32[]{:S(2)}) collective-permute-start(s16[3,128,128]{2,1,0:T(8,128)(2,1)S(1)} %param.15), channel_id=1, source_target_pairs={{224,240},{225,241},{226,242},{227,243},{228,244},{229,245},{230,2... | collective-permute-start | bytes 294920 | tf_op jit(solution)/shard_map/while/body/cond/branch_15_fun/ppermute | solution.py:387
  220.3 1.2 collective-permute-start.32
  221.5 4.0 %collective-permute-start.33 = (f32[16,4,128]{2,1,0:T(4,128)S(1)}, f32[16,4,128]{2,1,0:T(4,128)S(1)}, u32[]{:S(2)}, u32[]{:S(2)}) collective-permute-start(f32[16,4,128]{2,1,0:T(4,128)S(1)} %add.37), channel_id=1, source_target_pairs={{0,2},{1,3},{2,0},{3,1},{4,6},{5,7},{6,4},{7,5},{8,10},{9,11},{10,... | collective-permute-start | bytes 98312 | tf_op jit(solution)/shard_map/ppermute | solution.py:411
  225.6 5.5 %collective-permute-start.34 = (f32[16,4,128]{2,1,0:T(4,128)S(1)}, f32[16,4,128]{2,1,0:T(4,128)S(1)}, u32[]{:S(2)}, u32[]{:S(2)}) collective-permute-start(f32[16,4,128]{2,1,0:T(4,128)S(1)} %add.38), channel_id=1, source_target_pairs={{0,4},{1,5},{2,6},{3,7},{4,0},{5,1},{6,2},{7,3},{8,12},{9,13},{10,... | collective-permute-start | bytes 98312 | tf_op jit(solution)/shard_map/ppermute | solution.py:411
  231.1 7.9 %collective-permute-start.35 = (f32[16,4,128]{2,1,0:T(4,128)S(1)}, f32[16,4,128]{2,1,0:T(4,128)S(1)}, u32[]{:S(2)}, u32[]{:S(2)}) collective-permute-start(f32[16,4,128]{2,1,0:T(4,128)S(1)} %add.39), channel_id=1, source_target_pairs={{0,8},{1,9},{2,10},{3,11},{4,12},{5,13},{6,14},{7,15},{8,0},{9,1},... | collective-permute-start | bytes 98312 | tf_op jit(solution)/shard_map/ppermute | solution.py:411
  244.7 23.8 %collective-permute-start.29 = (s16[3,128,128]{2,1,0:T(8,128)(2,1)S(1)}, s16[3,128,128]{2,1,0:T(8,128)(2,1)S(1)}, u32[]{:S(2)}, u32[]{:S(2)}) collective-permute-start(s16[3,128,128]{2,1,0:T(8,128)(2,1)S(1)} %param.35), channel_id=1, source_target_pairs={{224,240},{225,241},{226,242},{227,243},{228,244},{229,245},{230,2... | collective-permute-start | bytes 294920 | tf_op jit(solution)/shard_map/while/body/cond/branch_15_fun/ppermute | solution.py:387
